TPU v7x, 256 devices: a whole 4x4x8 slice. The times are simulated.
256 devices in a mesh: row: 16 (over y_hi, x, core), col: 16 (over y_lo, z).
Axes of the slice: x: 4, y: 4 (y_hi: 2, y_lo: 2; y = y_hi * 2 + y_lo), z: 8, core: 2. Of those that a mesh axis runs over, the one named last changes fastest.
Arguments:
- x_blocks: bfloat16 [16, 16, 16, 128, 128], P('row', 'col'), may hold values from -0.8984375 to 0.8984375
- x_live: int32 [16, 16, 16], P('row', 'col'), may hold values 0 or 1
- pair_slots: int32 [16, 16, 4, 3, 192], P('row', 'col'), may hold values from 0 to 15
- pair_count: int32 [16, 16, 4], P('row', 'col'), may hold values from 15 to 192, as said below
Outputs:
- gram_blocks: float32 [16, 16, 16, 128, 128], P('row', 'col')
Inputs may be any that keep to these rules, and one draw needn't show every extreme that they name: `pair_count`: live pairs of a tile at a section; some tile has exactly 192 at its first section.
All inputs are finite; a program needn't handle non-finite values. No bound on the sum of `x_live` on one device may be relied on, other than what follows from the above.
Results may differ from a plain program's by a relative error of at most 0.0003.
Values may be sent and summed in bfloat16 or wider, within the bound.
A program may use at most 64 MiB of HBM per device.

v0:
```python
import jax
import jax.numpy as jnp
from jax import lax
from jax.sharding import PartitionSpec as P

SECTIONS = 4


def swapped_2(value, axis, distance):
    return lax.ppermute(value, axis, [(i, i ^ 1 << distance) for i in range(lax.axis_size(axis))])


def from_behind(value, axis, by):
    length = lax.axis_size(axis)
    return lax.ppermute(value, axis, [(i, (i + by) % length) for i in range(length)])


def add_pairs(gram_sum, left_piece, right_piece, picked, live_pairs):
    block_size = 48
    block_total = picked.shape[1] // block_size
    slot_total = left_piece.shape[0]
    slot_ids = lax.iota(jnp.int32, slot_total)

    def one_block(block_no, running):
        first_pair = block_no * block_size
        chosen = lax.dynamic_slice_in_dim(picked, first_pair, block_size, 1)
        positions = first_pair + lax.iota(jnp.int32, block_size)
        weights = (positions < live_pairs).astype(jnp.float32)
        left_pick = (chosen[0][:, None] == slot_ids[None, :]).astype(jnp.bfloat16)
        right_pick = (chosen[1][:, None] == slot_ids[None, :]).astype(jnp.bfloat16)
        out_pick = (chosen[2][:, None] == slot_ids[None, :]).astype(jnp.float32) * weights[:, None]
        left_rows = jnp.einsum(
            "ps,sik->pik", left_pick, left_piece, preferred_element_type=jnp.float32
        ).astype(jnp.bfloat16)
        right_rows = jnp.einsum(
            "ps,sjk->pjk", right_pick, right_piece, preferred_element_type=jnp.float32
        ).astype(jnp.bfloat16)
        product = jnp.einsum(
            "pik,pjk->pij", left_rows, right_rows, preferred_element_type=jnp.float32
        )
        added = jnp.einsum("po,pij->oij", out_pick, product, precision=lax.Precision.HIGHEST)
        return running + added

    return lax.fori_loop(0, block_total, one_block, gram_sum)


def body(x_blocks, x_live, pair_slots, pair_count):
    row_total = lax.axis_size("row")
    col_total = lax.axis_size("col")
    layers = row_total // col_total
    col_bits = col_total.bit_length() - 1
    layer_bits = layers.bit_length() - 1
    row_here = lax.axis_index("row")
    col_here = lax.axis_index("col")
    panel_here = row_here // layers
    tile_slots = x_blocks.shape[2]
    block_side = x_blocks.shape[3]
    filtered = x_blocks[0, 0] * x_live[0, 0].astype(jnp.bfloat16)[:, None, None]
    mirrored = filtered
    for bit_no in range(col_bits):
        swapped = swapped_2(mirrored, "row", bit_no + layer_bits)
        swapped = swapped_2(swapped, "col", bit_no)
        differ = panel_here // 2**bit_no % 2 != col_here // 2**bit_no % 2
        mirrored = jnp.where(differ, swapped, mirrored)
    gram_sum = jnp.zeros((tile_slots, block_side, block_side), jnp.float32)
    left_piece = filtered
    right_piece = mirrored
    for section_no in range(SECTIONS):
        if section_no > 0:
            left_piece = from_behind(left_piece, "col", -1)
            right_piece = from_behind(right_piece, "row", -layers)
        gram_sum = add_pairs(
            gram_sum,
            left_piece,
            right_piece,
            pair_slots[0, 0, section_no],
            pair_count[0, 0, section_no],
        )
    return gram_sum[None, None]


def solution(mesh):
    return jax.shard_map(
        body,
        mesh=mesh,
        in_specs=(
            P("row", "col", None, None, None),
            P("row", "col", None),
            P("row", "col", None, None, None),
            P("row", "col", None),
        ),
        out_specs=P("row", "col", None, None, None),
        check_vma=False,
    )
```

profile of v0, /device:TPU:239, one launch (start us, length us, event | category | flops | bytes accessed | tf_op | source)
XLA Modules:
  0.0 300.6 jit_solution(13352232010027332808)
XLA Ops:
  4.8 12.4 %collective-permute-done.1 = bf16[16,128,128]{2,1,0:T(8,128)(2,1)S(1)} collective-permute-done((bf16[16,128,128]{2,1,0:T(8,128)(2,1)S(1)}, bf16[16,128,128]{2,1,0:T(8,128)(2,1)S(1)}, u32[]{:S(2)}, u32[]{:S(2)}) %collective-permute-start.1) | collective-permute-done | bytes 524320 | tf_op jit(solution)/shard_map/ppermute | solution.py:10
  19.0 11.7 %collective-permute-done.2 = bf16[16,128,128]{2,1,0:T(8,128)(2,1)S(1)} collective-permute-done((bf16[16,128,128]{2,1,0:T(8,128)(2,1)S(1)}, bf16[16,128,128]{2,1,0:T(8,128)(2,1)S(1)}, u32[]{:S(2)}, u32[]{:S(2)}) %collective-permute-start.2) | collective-permute-done | bytes 524320 | tf_op jit(solution)/shard_map/ppermute | solution.py:10
  31.9 24.4 %collective-permute-done.3 = bf16[16,128,128]{2,1,0:T(8,128)(2,1)S(1)} collective-permute-done((bf16[16,128,128]{2,1,0:T(8,128)(2,1)S(1)}, bf16[16,128,128]{2,1,0:T(8,128)(2,1)S(1)}, u32[]{:S(2)}, u32[]{:S(2)}) %collective-permute-start.3) | collective-permute-done | bytes 524320 | tf_op jit(solution)/shard_map/ppermute | solution.py:10
  57.5 12.9 %collective-permute-done.4 = bf16[16,128,128]{2,1,0:T(8,128)(2,1)S(1)} collective-permute-done((bf16[16,128,128]{2,1,0:T(8,128)(2,1)S(1)}, bf16[16,128,128]{2,1,0:T(8,128)(2,1)S(1)}, u32[]{:S(2)}, u32[]{:S(2)}) %collective-permute-start.4) | collective-permute-done | bytes 524320 | tf_op jit(solution)/shard_map/ppermute | solution.py:10
  72.4 25.6 %collective-permute-done.5 = bf16[16,128,128]{2,1,0:T(8,128)(2,1)S(1)} collective-permute-done((bf16[16,128,128]{2,1,0:T(8,128)(2,1)S(1)}, bf16[16,128,128]{2,1,0:T(8,128)(2,1)S(1)}, u32[]{:S(2)}, u32[]{:S(2)}) %collective-permute-start.5) | collective-permute-done | bytes 524320 | tf_op jit(solution)/shard_map/ppermute | solution.py:10
  100.2 7.7 %collective-permute-done.8 = bf16[16,128,128]{2,1,0:T(8,128)(2,1)S(1)} collective-permute-done((bf16[16,128,128]{2,1,0:T(8,128)(2,1)S(1)}, bf16[16,128,128]{2,1,0:T(8,128)(2,1)S(1)}, u32[]{:S(2)}, u32[]{:S(2)}) %collective-permute-start.8) | collective-permute-done | bytes 524320 | tf_op jit(solution)/shard_map/ppermute | solution.py:15
  108.4 23.8 %collective-permute-done.6 = bf16[16,128,128]{2,1,0:T(8,128)(2,1)} collective-permute-done((bf16[16,128,128]{2,1,0:T(8,128)(2,1)S(1)}, bf16[16,128,128]{2,1,0:T(8,128)(2,1)}, u32[]{:S(2)}, u32[]{:S(2)}) %collective-permute-start.6) | collective-permute-done | bytes 524320 | tf_op jit(solution)/shard_map/ppermute | solution.py:10
  134.1 22.7 %collective-permute-done.7 = bf16[16,128,128]{2,1,0:T(8,128)(2,1)} collective-permute-done((bf16[16,128,128]{2,1,0:T(8,128)(2,1)}, bf16[16,128,128]{2,1,0:T(8,128)(2,1)}, u32[]{:S(2)}, u32[]{:S(2)}) %collective-permute-start.7) | collective-permute-done | bytes 524320 | tf_op jit(solution)/shard_map/ppermute | solution.py:10
  160.0 44.5 %while.63 = (s32[]{:T(128)}, f32[16,128,128]{2,0,1:T(8,128)S(1)}, s32[3,192]{1,0:T(4,128)S(1)}, s32[]{:T(128)}, bf16[16,128,128]{2,1,0:T(8,128)(2,1)S(1)}, /*ind...) while((s32[]{:T(128)}, f32[16,128,128]{2,0,1:T(8,128)S(1)}, ...), condition=%wide.region_1.2_spmd.clone.clone, body=%wide.region_0.1_spmd.clone.clone.sunk | while | flops 403180672 | bytes 15732073 | solution.py:44
  162.4 2.8 fusion.176
  165.8 5.3 %fusion.177 = f32[16,128,128]{2,0,1:T(8,128)S(1)} fusion(f32[48,128,128]{2,1,0:T(8,128)} %fusion.176, f32[16,128,128]{2,0,1:T(8,128)S(1)} %get-tuple-element.921, pred[]{:T(512)S(6)} %compare.26, f32[48]{0:T(128)S(1)} %compare_convert_fusion.11, s32[48]{0:T(128)S(1)} %get-tuple-element.909), kind=kOutput, calls=%fused_computation.93.clone.1 | convolution fusion | flops 151520768 | bytes 5243265 | tf_op jit(solution)/shard_map/while/body/eval_jaxpr/po,pij->oij/dot_general | solution.py:41
  173.6 2.8 fusion.176
  177.0 5.3 %fusion.177 = f32[16,128,128]{2,0,1:T(8,128)S(1)} fusion(f32[48,128,128]{2,1,0:T(8,128)} %fusion.176, f32[16,128,128]{2,0,1:T(8,128)S(1)} %get-tuple-element.921, pred[]{:T(512)S(6)} %compare.26, f32[48]{0:T(128)S(1)} %compare_convert_fusion.11, s32[48]{0:T(128)S(1)} %get-tuple-element.909), kind=kOutput, calls=%fused_computation.93.clone.1 | convolution fusion | flops 151520768 | bytes 5243265 | tf_op jit(solution)/shard_map/while/body/eval_jaxpr/po,pij->oij/dot_general | solution.py:41
  184.7 2.8 fusion.176
  188.1 5.3 %fusion.177 = f32[16,128,128]{2,0,1:T(8,128)S(1)} fusion(f32[48,128,128]{2,1,0:T(8,128)} %fusion.176, f32[16,128,128]{2,0,1:T(8,128)S(1)} %get-tuple-element.921, pred[]{:T(512)S(6)} %compare.26, f32[48]{0:T(128)S(1)} %compare_convert_fusion.11, s32[48]{0:T(128)S(1)} %get-tuple-element.909), kind=kOutput, calls=%fused_computation.93.clone.1 | convolution fusion | flops 151520768 | bytes 5243265 | tf_op jit(solution)/shard_map/while/body/eval_jaxpr/po,pij->oij/dot_general | solution.py:41
  195.8 2.8 fusion.176
  199.2 5.3 %fusion.177 = f32[16,128,128]{2,0,1:T(8,128)S(1)} fusion(f32[48,128,128]{2,1,0:T(8,128)} %fusion.176, f32[16,128,128]{2,0,1:T(8,128)S(1)} %get-tuple-element.921, pred[]{:T(512)S(6)} %compare.26, f32[48]{0:T(128)S(1)} %compare_convert_fusion.11, s32[48]{0:T(128)S(1)} %get-tuple-element.909), kind=kOutput, calls=%fused_computation.93.clone.1 | convolution fusion | flops 151520768 | bytes 5243265 | tf_op jit(solution)/shard_map/while/body/eval_jaxpr/po,pij->oij/dot_general | solution.py:41
  204.6 31.3 %while.60 = (s32[]{:T(128)}, f32[16,128,128]{2,0,1:T(8,128)S(1)}, s32[3,192]{1,0:T(4,128)S(1)}, s32[]{:T(128)}, bf16[16,128,128]{2,1,0:T(8,128)(2,1)S(1)}, /*ind...) while((s32[]{:T(128)}, f32[16,128,128]{2,0,1:T(8,128)S(1)}, ...), condition=%wide.region_3.4_spmd.clone.clone, body=%wide.region_2.3_spmd.clone.clone.sunk | while | flops 402918528 | bytes 15732063 | solution.py:44
  209.0 3.5 %fusion.147 = f32[16,128,128]{2,0,1:T(8,128)S(1)} fusion(f32[16,128,128]{2,0,1:T(8,128)S(1)} %get-tuple-element.951, f32[48,128,128]{2,1,0:T(8,128)S(1)} %fusion.146, f32[48]{0:T(128)S(1)} %compare_convert_fusion.8, s32[48]{0:T(128)S(1)} %get-tuple-element.882), kind=kOutput, calls=%fused_computation.9.clone.1 | convolution fusion | flops 151258624 | bytes 5243264 | tf_op jit(solution)/shard_map/while/body/eval_jaxpr/po,pij->oij/dot_general | solution.py:41
  216.8 3.5 %fusion.147 = f32[16,128,128]{2,0,1:T(8,128)S(1)} fusion(f32[16,128,128]{2,0,1:T(8,128)S(1)} %get-tuple-element.951, f32[48,128,128]{2,1,0:T(8,128)S(1)} %fusion.146, f32[48]{0:T(128)S(1)} %compare_convert_fusion.8, s32[48]{0:T(128)S(1)} %get-tuple-element.882), kind=kOutput, calls=%fused_computation.9.clone.1 | convolution fusion | flops 151258624 | bytes 5243264 | tf_op jit(solution)/shard_map/while/body/eval_jaxpr/po,pij->oij/dot_general | solution.py:41
  224.6 3.5 %fusion.147 = f32[16,128,128]{2,0,1:T(8,128)S(1)} fusion(f32[16,128,128]{2,0,1:T(8,128)S(1)} %get-tuple-element.951, f32[48,128,128]{2,1,0:T(8,128)S(1)} %fusion.146, f32[48]{0:T(128)S(1)} %compare_convert_fusion.8, s32[48]{0:T(128)S(1)} %get-tuple-element.882), kind=kOutput, calls=%fused_computation.9.clone.1 | convolution fusion | flops 151258624 | bytes 5243264 | tf_op jit(solution)/shard_map/while/body/eval_jaxpr/po,pij->oij/dot_general | solution.py:41
  232.5 3.5 %fusion.147 = f32[16,128,128]{2,0,1:T(8,128)S(1)} fusion(f32[16,128,128]{2,0,1:T(8,128)S(1)} %get-tuple-element.951, f32[48,128,128]{2,1,0:T(8,128)S(1)} %fusion.146, f32[48]{0:T(128)S(1)} %compare_convert_fusion.8, s32[48]{0:T(128)S(1)} %get-tuple-element.882), kind=kOutput, calls=%fused_computation.9.clone.1 | convolution fusion | flops 151258624 | bytes 5243264 | tf_op jit(solution)/shard_map/while/body/eval_jaxpr/po,pij->oij/dot_general | solution.py:41
  237.2 35.3 %while.61 = (s32[]{:T(128)}, f32[16,128,128]{2,0,1:T(8,128)S(1)}, s32[3,192]{1,0:T(4,128)S(1)}, s32[]{:T(128)}, bf16[16,128,128]{2,1,0:T(8,128)(2,1)}, /*index=5...) while((s32[]{:T(128)}, f32[16,128,128]{2,0,1:T(8,128)S(1)}, ...), condition=%wide.region_5.6_spmd.clone.clone, body=%wide.region_4.5_spmd.clone.clone.sunk | while | flops 402918528 | bytes 15732063 | solution.py:44
  242.5 3.5 %fusion.157 = f32[16,128,128]{2,0,1:T(8,128)S(1)} fusion(f32[16,128,128]{2,0,1:T(8,128)S(1)} %get-tuple-element.981, f32[48,128,128]{2,1,0:T(8,128)S(1)} %fusion.156, f32[48]{0:T(128)S(1)} %compare_convert_fusion.9, s32[48]{0:T(128)S(1)} %get-tuple-element.891), kind=kOutput, calls=%fused_computation.37.clone.1 | convolution fusion | flops 151258624 | bytes 5243264 | tf_op jit(solution)/shard_map/while/body/eval_jaxpr/po,pij->oij/dot_general | solution.py:41
  251.3 3.5 %fusion.157 = f32[16,128,128]{2,0,1:T(8,128)S(1)} fusion(f32[16,128,128]{2,0,1:T(8,128)S(1)} %get-tuple-element.981, f32[48,128,128]{2,1,0:T(8,128)S(1)} %fusion.156, f32[48]{0:T(128)S(1)} %compare_convert_fusion.9, s32[48]{0:T(128)S(1)} %get-tuple-element.891), kind=kOutput, calls=%fused_computation.37.clone.1 | convolution fusion | flops 151258624 | bytes 5243264 | tf_op jit(solution)/shard_map/while/body/eval_jaxpr/po,pij->oij/dot_general | solution.py:41
  260.1 3.5 %fusion.157 = f32[16,128,128]{2,0,1:T(8,128)S(1)} fusion(f32[16,128,128]{2,0,1:T(8,128)S(1)} %get-tuple-element.981, f32[48,128,128]{2,1,0:T(8,128)S(1)} %fusion.156, f32[48]{0:T(128)S(1)} %compare_convert_fusion.9, s32[48]{0:T(128)S(1)} %get-tuple-element.891), kind=kOutput, calls=%fused_computation.37.clone.1 | convolution fusion | flops 151258624 | bytes 5243264 | tf_op jit(solution)/shard_map/while/body/eval_jaxpr/po,pij->oij/dot_general | solution.py:41
  268.9 3.5 %fusion.157 = f32[16,128,128]{2,0,1:T(8,128)S(1)} fusion(f32[16,128,128]{2,0,1:T(8,128)S(1)} %get-tuple-element.981, f32[48,128,128]{2,1,0:T(8,128)S(1)} %fusion.156, f32[48]{0:T(128)S(1)} %compare_convert_fusion.9, s32[48]{0:T(128)S(1)} %get-tuple-element.891), kind=kOutput, calls=%fused_computation.37.clone.1 | convolution fusion | flops 151258624 | bytes 5243264 | tf_op jit(solution)/shard_map/while/body/eval_jaxpr/po,pij->oij/dot_general | solution.py:41
  272.4 26.9 %while.62 = (s32[]{:T(128)}, f32[16,128,128]{2,0,1:T(8,128)S(1)}, s32[3,192]{1,0:T(4,128)S(1)}, s32[]{:T(128)}, bf16[16,128,128]{2,1,0:T(8,128)(2,1)S(1)}, /*ind...) while((s32[]{:T(128)}, f32[16,128,128]{2,0,1:T(8,128)S(1)}, ...), condition=%wide.region_7.8_spmd.clone.clone, body=%wide.region_6.7_spmd.clone.clone.sunk | while | flops 402918528 | bytes 15732063 | solution.py:44
  275.7 3.5 %fusion.167 = f32[16,128,128]{2,0,1:T(8,128)S(1)} fusion(f32[16,128,128]{2,0,1:T(8,128)S(1)} %get-tuple-element.1011, f32[48,128,128]{2,1,0:T(8,128)S(1)} %fusion.166, f32[48]{0:T(128)S(1)} %compare_convert_fusion.10, s32[48]{0:T(128)S(1)} %get-tuple-element.900), kind=kOutput, calls=%fused_computation.65.clone.1 | convolution fusion | flops 151258624 | bytes 5243264 | tf_op jit(solution)/shard_map/while/body/eval_jaxpr/po,pij->oij/dot_general | solution.py:41
  282.4 3.5 %fusion.167 = f32[16,128,128]{2,0,1:T(8,128)S(1)} fusion(f32[16,128,128]{2,0,1:T(8,128)S(1)} %get-tuple-element.1011, f32[48,128,128]{2,1,0:T(8,128)S(1)} %fusion.166, f32[48]{0:T(128)S(1)} %compare_convert_fusion.10, s32[48]{0:T(128)S(1)} %get-tuple-element.900), kind=kOutput, calls=%fused_computation.65.clone.1 | convolution fusion | flops 151258624 | bytes 5243264 | tf_op jit(solution)/shard_map/while/body/eval_jaxpr/po,pij->oij/dot_general | solution.py:41
  289.1 3.5 %fusion.167 = f32[16,128,128]{2,0,1:T(8,128)S(1)} fusion(f32[16,128,128]{2,0,1:T(8,128)S(1)} %get-tuple-element.1011, f32[48,128,128]{2,1,0:T(8,128)S(1)} %fusion.166, f32[48]{0:T(128)S(1)} %compare_convert_fusion.10, s32[48]{0:T(128)S(1)} %get-tuple-element.900), kind=kOutput, calls=%fused_computation.65.clone.1 | convolution fusion | flops 151258624 | bytes 5243264 | tf_op jit(solution)/shard_map/while/body/eval_jaxpr/po,pij->oij/dot_general | solution.py:41
  295.8 3.5 %fusion.167 = f32[16,128,128]{2,0,1:T(8,128)S(1)} fusion(f32[16,128,128]{2,0,1:T(8,128)S(1)} %get-tuple-element.1011, f32[48,128,128]{2,1,0:T(8,128)S(1)} %fusion.166, f32[48]{0:T(128)S(1)} %compare_convert_fusion.10, s32[48]{0:T(128)S(1)} %get-tuple-element.900), kind=kOutput, calls=%fused_computation.65.clone.1 | convolution fusion | flops 151258624 | bytes 5243264 | tf_op jit(solution)/shard_map/while/body/eval_jaxpr/po,pij->oij/dot_general | solution.py:41
  (130 shorter events, 84.5 us)
Async XLA Ops:
  1.8 2.3 collective-permute-start
  4.1 13.1 %collective-permute-start.1 = (bf16[16,128,128]{2,1,0:T(8,128)(2,1)S(1)}, bf16[16,128,128]{2,1,0:T(8,128)(2,1)S(1)}, u32[]{:S(2)}, u32[]{:S(2)}) collective-permute-start(bf16[16,128,128]{2,1,0:T(8,128)(2,1)S(1)} %collective-permute-done), channel_id=1, source_target_pairs={{0,1},{1,0},{2,3},{3,2},{4,5},{5,4},{6,7},{7,6},{8,9},{9,8},{10,11... | collective-permute-start | bytes 1572872 | tf_op jit(solution)/shard_map/ppermute | solution.py:10
  18.4 12.3 %collective-permute-start.2 = (bf16[16,128,128]{2,1,0:T(8,128)(2,1)S(1)}, bf16[16,128,128]{2,1,0:T(8,128)(2,1)S(1)}, u32[]{:S(2)}, u32[]{:S(2)}) collective-permute-start(bf16[16,128,128]{2,1,0:T(8,128)(2,1)S(1)} %broadcast_select_fusion), channel_id=1, source_target_pairs={{0,32},{16,48},{32,0},{48,16},{64,96},{80,112},{96,64},{112,80},{1... | collective-permute-start | bytes 1572872 | tf_op jit(solution)/shard_map/ppermute | solution.py:10
  30.7 25.5 %collective-permute-start.3 = (bf16[16,128,128]{2,1,0:T(8,128)(2,1)S(1)}, bf16[16,128,128]{2,1,0:T(8,128)(2,1)S(1)}, u32[]{:S(2)}, u32[]{:S(2)}) collective-permute-start(bf16[16,128,128]{2,1,0:T(8,128)(2,1)S(1)} %collective-permute-done.2), channel_id=1, source_target_pairs={{0,2},{1,3},{2,0},{3,1},{4,6},{5,7},{6,4},{7,5},{8,10},{9,11},{10,... | collective-permute-start | bytes 1572872 | tf_op jit(solution)/shard_map/ppermute | solution.py:10
  31.9 101.4 %copy-start = (s32[1,1,4,3,192]{4,2,3,1,0:T(4,128)S(1)}, s32[1,1,4,3,192]{4,2,3,1,0:T(4,128)}, u32[]{:S(2)}) copy-start(s32[1,1,4,3,192]{4,2,3,1,0:T(4,128)} %param.14) | copy-start | bytes 27652
  31.9 101.5 %copy-start.1 = (s32[1,1,4]{2,1,0:T(1,128)S(1)}, s32[1,1,4]{2,1,0:T(1,128)}, u32[]{:S(2)}) copy-start(s32[1,1,4]{2,1,0:T(1,128)} %param.15) | copy-start | bytes 52
  56.3 14.1 %collective-permute-start.4 = (bf16[16,128,128]{2,1,0:T(8,128)(2,1)S(1)}, bf16[16,128,128]{2,1,0:T(8,128)(2,1)S(1)}, u32[]{:S(2)}, u32[]{:S(2)}) collective-permute-start(bf16[16,128,128]{2,1,0:T(8,128)(2,1)S(1)} %broadcast_select_fusion.1), channel_id=1, source_target_pairs={{0,64},{16,80},{32,96},{48,112},{64,0},{80,16},{96,32},{112,48},{1... | collective-permute-start | bytes 1572872 | tf_op jit(solution)/shard_map/ppermute | solution.py:10
  70.4 27.6 %collective-permute-start.5 = (bf16[16,128,128]{2,1,0:T(8,128)(2,1)S(1)}, bf16[16,128,128]{2,1,0:T(8,128)(2,1)S(1)}, u32[]{:S(2)}, u32[]{:S(2)}) collective-permute-start(bf16[16,128,128]{2,1,0:T(8,128)(2,1)S(1)} %collective-permute-done.4), channel_id=1, source_target_pairs={{0,4},{1,5},{2,6},{3,7},{4,0},{5,1},{6,2},{7,3},{8,12},{9,13},{10,... | collective-permute-start | bytes 1572872 | tf_op jit(solution)/shard_map/ppermute | solution.py:10
  72.4 35.5 %collective-permute-start.8 = (bf16[16,128,128]{2,1,0:T(8,128)(2,1)S(1)}, bf16[16,128,128]{2,1,0:T(8,128)(2,1)S(1)}, u32[]{:S(2)}, u32[]{:S(2)}) collective-permute-start(bf16[16,128,128]{2,1,0:T(8,128)(2,1)S(1)} %bitcast_multiply_fusion), channel_id=1, source_target_pairs={{0,15},{1,0},{2,1},{3,2},{4,3},{5,4},{6,5},{7,6},{8,7},{9,8},{10,9... | collective-permute-start | bytes 1572872 | tf_op jit(solution)/shard_map/ppermute | solution.py:15
  98.1 34.1 %collective-permute-start.6 = (bf16[16,128,128]{2,1,0:T(8,128)(2,1)S(1)}, bf16[16,128,128]{2,1,0:T(8,128)(2,1)}, u32[]{:S(2)}, u32[]{:S(2)}) collective-permute-start(bf16[16,128,128]{2,1,0:T(8,128)(2,1)S(1)} %broadcast_select_fusion.2), channel_id=1, source_target_pairs={{0,128},{16,144},{32,160},{48,176},{64,192},{80,208},{96,224},{112... | collective-permute-start | bytes 1572872 | tf_op jit(solution)/shard_map/ppermute | solution.py:10
  107.9 26.2 %collective-permute-start.10 = (bf16[16,128,128]{2,1,0:T(8,128)(2,1)S(1)}, bf16[16,128,128]{2,1,0:T(8,128)(2,1)}, u32[]{:S(2)}, u32[]{:S(2)}) collective-permute-start(bf16[16,128,128]{2,1,0:T(8,128)(2,1)S(1)} %collective-permute-done.8), channel_id=1, source_target_pairs={{0,15},{1,0},{2,1},{3,2},{4,3},{5,4},{6,5},{7,6},{8,7},{9,8},{10,9... | collective-permute-start | bytes 1572872 | tf_op jit(solution)/shard_map/ppermute | solution.py:15
  132.2 24.5 %collective-permute-start.7 = (bf16[16,128,128]{2,1,0:T(8,128)(2,1)}, bf16[16,128,128]{2,1,0:T(8,128)(2,1)}, u32[]{:S(2)}, u32[]{:S(2)}) collective-permute-start(bf16[16,128,128]{2,1,0:T(8,128)(2,1)} %collective-permute-done.6), channel_id=1, source_target_pairs={{0,8},{1,9},{2,10},{3,11},{4,12},{5,13},{6,14},{7,15},{8,0},{9,1},... | collective-permute-start | bytes 1572872 | tf_op jit(solution)/shard_map/ppermute | solution.py:10
  134.1 138.4 %collective-permute-start.12 = (bf16[16,128,128]{2,1,0:T(8,128)(2,1)}, bf16[16,128,128]{2,1,0:T(8,128)(2,1)S(1)}, u32[]{:S(2)}, u32[]{:S(2)}) collective-permute-start(bf16[16,128,128]{2,1,0:T(8,128)(2,1)} %collective-permute-done.10), channel_id=1, source_target_pairs={{0,15},{1,0},{2,1},{3,2},{4,3},{5,4},{6,5},{7,6},{8,7},{9,8},{10,9... | collective-permute-start | bytes 1572872 | tf_op jit(solution)/shard_map/ppermute | solution.py:15
  158.6 45.9 %collective-permute-start.9 = (bf16[16,128,128]{2,1,0:T(8,128)(2,1)}, bf16[16,128,128]{2,1,0:T(8,128)(2,1)}, u32[]{:S(2)}, u32[]{:S(2)}) collective-permute-start(bf16[16,128,128]{2,1,0:T(8,128)(2,1)} %broadcast_select_fusion.3), channel_id=1, source_target_pairs={{0,240},{16,0},{32,16},{48,32},{64,48},{80,64},{96,80},{112,96},{1... | collective-permute-start | bytes 1572872 | tf_op jit(solution)/shard_map/ppermute | solution.py:15
  204.5 31.4 %collective-permute-start.11 = (bf16[16,128,128]{2,1,0:T(8,128)(2,1)}, bf16[16,128,128]{2,1,0:T(8,128)(2,1)}, u32[]{:S(2)}, u32[]{:S(2)}) collective-permute-start(bf16[16,128,128]{2,1,0:T(8,128)(2,1)} %collective-permute-done.9), channel_id=1, source_target_pairs={{0,240},{16,0},{32,16},{48,32},{64,48},{80,64},{96,80},{112,96},{1... | collective-permute-start | bytes 1572872 | tf_op jit(solution)/shard_map/ppermute | solution.py:15
  235.9 36.5 %collective-permute-start.13 = (bf16[16,128,128]{2,1,0:T(8,128)(2,1)}, bf16[16,128,128]{2,1,0:T(8,128)(2,1)S(1)}, u32[]{:S(2)}, u32[]{:S(2)}) collective-permute-start(bf16[16,128,128]{2,1,0:T(8,128)(2,1)} %collective-permute-done.11), channel_id=1, source_target_pairs={{0,240},{16,0},{32,16},{48,32},{64,48},{80,64},{96,80},{112,96},{1... | collective-permute-start | bytes 1572872 | tf_op jit(solution)/shard_map/ppermute | solution.py:15
where the time goes:
time: 305 us; the launch traced here: 301 us
  waiting for transfers between devices  143 us (47%)
  matrix products  126 us (41%)
  other arithmetic  14.9 us (5%)
  starting transfers between devices  12.8 us (4%)
  local copies, waits for them, and re-layouts  3.32 us (1%)
    ppermute x8, waiting for transfers between devices, swapped_2(): lax.ppermute(value, axis, [(i, i ^ 1 << distance) for i in range(lax.axis...  135 us
    dot_general x16, matrix products, one_block(): jnp.einsum('po,pij->oij', out_pick, product, precision=lax.Precision.HIGH...  62.5 us
    dot_general x16, matrix products, one_block(): jnp.einsum('pik,pjk->pij', left_rows, right_rows, preferred_element_type=...  25.9 us
    dot_general x16, matrix products, one_block(): jnp.einsum('ps,sjk->pjk', right_pick, right_piece, preferred_element_type...  22.9 us
    dot_general x16, matrix products, one_block(): jnp.einsum('ps,sik->pik', left_pick, left_piece, preferred_element_type=j...  14.5 us
    convert_element_type x16, other arithmetic, one_block(): weights = (positions < live_pairs).astype(jnp.float32)  9.97 us
    ppermute x8, starting transfers between devices, swapped_2(): lax.ppermute(value, axis, [(i, i ^ 1 << distance) for i in range(lax.axis...  9.66 us
    ppermute x6, waiting for transfers between devices, from_behind(): lax.ppermute(value, axis, [(i, (i + by) % length) for i in range(length)])  7.7 us
  transfers between devices with their start and end apart: 14, of which 9 were waited for; matrix products, arithmetic and copies ran while one was open for 38% of the time, Pallas kernels for 0%

commit v1 on v0

v1 whole, which is shorter than its diff:
```python
import functools

import jax
import jax.numpy as jnp
from jax import lax
from jax.experimental import pallas as pl
from jax.experimental.pallas import tpu as pltpu
from jax.sharding import PartitionSpec as P

SECTIONS = 4
SLOTS = 16
BLK = 128
PAIRS = 192
SIDE = 16
RING = 8
CHUNKS = 4
GROUP = 8
LISTED = 896
MESH = pl.DeviceIdType.MESH


def make_list(pairs, counts, left_live, right_live, listed, spans):
    slot_ids = lax.broadcasted_iota(jnp.int32, (SLOTS, PAIRS), 0)
    lanes = lax.broadcasted_iota(jnp.int32, (1, PAIRS), 1)
    earlier = (
        lax.broadcasted_iota(jnp.int32, (PAIRS, PAIRS), 0)
        < lax.broadcasted_iota(jnp.int32, (PAIRS, PAIRS), 1)
    ).astype(jnp.float32).astype(jnp.bfloat16)

    def hot(row):
        return (slot_ids == row).astype(jnp.float32)

    def look_up(live, row):
        table = jnp.broadcast_to(live.astype(jnp.float32), (8, SLOTS)).astype(jnp.bfloat16)
        return jnp.dot(
            table, hot(row).astype(jnp.bfloat16), preferred_element_type=jnp.float32
        )[0:1]

    chosen, places, totals = [], [], jnp.zeros((SLOTS, 1), jnp.float32)
    for s in range(SECTIONS):
        left, right, out = (pairs[s, k : k + 1, :] for k in range(3))
        used = look_up(left_live[s], left) * look_up(right_live[s], right)
        used = jnp.where(lanes < counts[s], used, 0.0)
        picked = hot(out) * used
        before = jnp.dot(picked.astype(jnp.bfloat16), earlier, preferred_element_type=jnp.float32)
        chosen.append(picked)
        places.append(before + totals)
        totals = totals + jnp.sum(picked, axis=1, keepdims=True)
    groups = jnp.floor((totals + (GROUP - 1)) * (1.0 / GROUP))
    below = (
        lax.broadcasted_iota(jnp.int32, (SLOTS, SLOTS), 1)
        < lax.broadcasted_iota(jnp.int32, (SLOTS, SLOTS), 0)
    ).astype(jnp.float32).astype(jnp.bfloat16)
    starts = jnp.dot(
        below,
        jnp.broadcast_to(groups, (SLOTS, BLK)).astype(jnp.bfloat16),
        preferred_element_type=jnp.float32,
    )
    lane = lax.broadcasted_iota(jnp.int32, (SLOTS, BLK), 1)
    spans[...] = jnp.where(lane == 0, starts, jnp.broadcast_to(groups, (SLOTS, BLK))).astype(jnp.int32)
    first = starts[:, 0:1] * GROUP
    gathered = jnp.zeros((8, LISTED), jnp.float32)
    positions = lax.broadcasted_iota(jnp.int32, (LISTED, PAIRS), 0).astype(jnp.float32)
    row_ids = lax.broadcasted_iota(jnp.int32, (8, PAIRS), 0)
    for s in range(SECTIONS):
        place = jnp.sum(chosen[s] * (places[s] + first + 1.0), axis=0, keepdims=True) - 1.0
        codes = jnp.where(row_ids == 0, pairs[s, 0:1, :], pairs[s, 1:2, :]) + (1 + SLOTS * s)
        gathered += lax.dot_general(
            codes.astype(jnp.float32).astype(jnp.bfloat16),
            (positions == place).astype(jnp.float32).astype(jnp.bfloat16),
            (((1,), (1,)), ((), ())),
            preferred_element_type=jnp.float32,
        )
    listed[...] = gathered.astype(jnp.int32)


def moves_kernel(
    x, live, pairs, counts, L, R, listed, spans,
    lv, rv, l_send, l_recv, r_send, r_recv, m_send, lv_send, lv_recv, rv_send, rv_recv, own_sem,
):
    a = lax.axis_index("row")
    b = lax.axis_index("col")

    def at(row, col):
        return (lax.rem(row + SIDE, SIDE), lax.rem(col + SIDE, SIDE))

    twin = a == b
    gap = lax.rem(lax.rem(b, RING) - lax.rem(a, RING) + RING, RING)
    back = lax.rem(RING - gap, RING)
    late = jnp.logical_or(back == 2, back == 3)
    step = jnp.where(late, 2, jnp.where(back == 1, 1, 0))
    out_0 = jnp.logical_or(gap == 0, gap >= 4)
    out_1 = gap == 0
    out_2 = gap <= 1
    not_twin = jnp.logical_not(twin)
    go_0 = jnp.logical_and(out_0, not_twin)

    barrier = pltpu.get_barrier_semaphore()

    def hello(device):
        pl.semaphore_signal(barrier, inc=1, device_id=device, device_id_type=MESH)

    hello(at(a, b + 1))
    hello(at(a + 1, b))
    hello(at(a + 2, b))

    @pl.when(not_twin)
    def _():
        hello(at(b, a))
        hello(at(b, a - step))

    one = jnp.int32(1)
    zero = jnp.int32(0)
    expected = (
        3
        + jnp.where(not_twin, one, zero)
        + jnp.where(go_0, one, zero)
        + jnp.where(out_1, one, zero)
        + jnp.where(out_2, one, zero)
    )
    pl.semaphore_wait(barrier, expected)

    size = SLOTS // CHUNKS

    def part(q):
        return pl.ds(q * size, size)

    def remote(src, dst, send, recv, device):
        return pltpu.make_async_remote_copy(
            src_ref=src, dst_ref=dst, send_sem=send, recv_sem=recv, device_id=device, device_id_type=MESH
        )

    def left(k, q):
        src = x.at[part(q)] if k == 0 else L.at[k - 1, part(q)]
        return remote(src, L.at[k, part(q)], l_send.at[k, q], l_recv.at[k, q], at(a, b - 1))

    def mirror(j, q):
        src = x.at[part(q)] if j == 0 else L.at[j - 1, part(q)]
        return remote(src, R.at[0, part(q)], m_send.at[j, q], r_recv.at[0, q], at(b + j, a))

    def right(k, q):
        src = R.at[2 if k == 3 else 0, part(q)]
        device = at(a - (2 if k == 2 else 1), b)
        return remote(src, R.at[k, part(q)], r_send.at[k, q], r_recv.at[k, q], device)

    def live_left(k):
        src = live if k == 0 else lv.at[k - 1]
        return remote(src, lv.at[k], lv_send.at[k], lv_recv.at[k], at(a, b - 1))

    def live_mirror(k):
        src = live if k == 0 else lv.at[k - 1]
        return remote(src, rv.at[k], rv_send.at[k], rv_recv.at[k], at(b, a))

    own = pltpu.make_async_copy(x, R.at[0], own_sem)

    live_left(0).start()

    @pl.when(not_twin)
    def _():
        live_mirror(0).start()

    @pl.when(twin)
    def _():
        own.start()

    for q in range(CHUNKS):
        left(0, q).start()

    @pl.when(go_0)
    def _():
        for q in range(CHUNKS):
            mirror(0, q).start()

    for k in range(3):
        live_left(k).wait_recv()
        if k < 2:
            live_left(k + 1).start()

        @pl.when(not_twin)
        def _():
            live_mirror(k + 1).start()

    @pl.when(not_twin)
    def _():
        for k in range(4):
            live_mirror(k).wait_recv()

    lefts = [live[...], lv[0], lv[1], lv[2]]
    rights = [jnp.where(twin, lefts[k], rv[k]) for k in range(4)]
    make_list(pairs, counts, lefts, rights, listed, spans)

    def take_mirror(q):
        @pl.when(not_twin)
        def _():
            mirror(0, q).wait_recv()

        right(1, q).start()
        right(2, q).start()

    def pass_on(q):
        right(2, q).wait_recv()
        right(3, q).start()

    for q in range(CHUNKS):
        left(0, q).wait_recv()
        left(1, q).start()

        @pl.when(out_1)
        def _():
            mirror(1, q).start()

    @pl.when(twin)
    def _():
        own.wait()

    for q in range(CHUNKS):
        @pl.when(late)
        def _():
            pass_on(q)

        @pl.when(jnp.logical_not(late))
        def _():
            take_mirror(q)

        left(1, q).wait_recv()
        left(2, q).start()

        @pl.when(out_2)
        def _():
            mirror(2, q).start()

    for q in range(CHUNKS):
        @pl.when(late)
        def _():
            take_mirror(q)

        @pl.when(jnp.logical_not(late))
        def _():
            pass_on(q)

    for q in range(CHUNKS):
        left(2, q).wait_recv()
        right(1, q).wait_recv()
        right(3, q).wait_recv()

    for q in range(CHUNKS):
        for k in range(3):
            left(k, q).wait_send()
            right(k + 1, q).wait_send()

        @pl.when(go_0)
        def _():
            mirror(0, q).wait_send()

        @pl.when(out_1)
        def _():
            mirror(1, q).wait_send()

        @pl.when(out_2)
        def _():
            mirror(2, q).wait_send()

    for k in range(3):
        live_left(k).wait_send()

    @pl.when(not_twin)
    def _():
        for k in range(4):
            live_mirror(k).wait_send()


def moves(x, live, pairs, counts):
    dma = pltpu.SemaphoreType.DMA
    tile = (SLOTS, BLK, BLK)
    return pl.pallas_call(
        moves_kernel,
        out_shape=[
            jax.ShapeDtypeStruct((3,) + tile, jnp.bfloat16),
            jax.ShapeDtypeStruct((4,) + tile, jnp.bfloat16),
            jax.ShapeDtypeStruct((8, LISTED), jnp.int32),
            jax.ShapeDtypeStruct((SLOTS, BLK), jnp.int32),
        ],
        in_specs=[
            pl.BlockSpec(memory_space=pl.ANY),
            pl.BlockSpec(memory_space=pltpu.VMEM),
            pl.BlockSpec(memory_space=pltpu.VMEM),
            pl.BlockSpec(memory_space=pltpu.SMEM),
        ],
        out_specs=[
            pl.BlockSpec(memory_space=pl.ANY),
            pl.BlockSpec(memory_space=pl.ANY),
            pl.BlockSpec(memory_space=pltpu.VMEM),
            pl.BlockSpec(memory_space=pltpu.VMEM),
        ],
        scratch_shapes=[
            pltpu.VMEM((3, 1, SLOTS), jnp.int32),
            pltpu.VMEM((4, 1, SLOTS), jnp.int32),
            dma((3, CHUNKS)), dma((3, CHUNKS)),
            dma((4, CHUNKS)), dma((4, CHUNKS)),
            dma((3, CHUNKS)),
            dma((3,)), dma((3,)), dma((4,)), dma((4,)),
            dma,
        ],
        compiler_params=pltpu.CompilerParams(collective_id=0, has_side_effects=True),
        name="moves",
    )(x, live, pairs, counts)


def sums_kernel(listed, spans, x, L, R, out, left, right, total, in_sems, out_sems):
    copies = [
        pltpu.make_async_copy(x, left.at[pl.ds(1, SLOTS)], in_sems.at[0]),
        pltpu.make_async_copy(L, left.at[pl.ds(1 + SLOTS, 3 * SLOTS)], in_sems.at[1]),
        pltpu.make_async_copy(R, right.at[pl.ds(1, 4 * SLOTS)], in_sems.at[2]),
    ]
    for c in copies:
        c.start()
    left[0] = jnp.zeros((BLK, BLK), jnp.bfloat16)
    right[0] = jnp.zeros((BLK, BLK), jnp.bfloat16)
    for c in copies:
        c.wait()

    def send(o):
        return pltpu.make_async_copy(total.at[o], out.at[o], out_sems.at[o])

    for o in range(SLOTS):
        start = spans[o, 0]

        def one_group(i, acc):
            base = (start + i) * GROUP
            for k in range(0, GROUP, 2):
                rows = jnp.concatenate([left[listed[0, base + k]], left[listed[0, base + k + 1]]], axis=1)
                cols = jnp.concatenate([right[listed[1, base + k]], right[listed[1, base + k + 1]]], axis=1)
                acc = acc + lax.dot_general(
                    rows, cols, (((1,), (1,)), ((), ())), preferred_element_type=jnp.float32
                )
            return acc

        total[o] = lax.fori_loop(0, spans[o, 1], one_group, jnp.zeros((BLK, BLK), jnp.float32))
        send(o).start()
    for o in range(SLOTS):
        send(o).wait()


def sums(listed, spans, x, L, R):
    return pl.pallas_call(
        sums_kernel,
        out_shape=jax.ShapeDtypeStruct((SLOTS, BLK, BLK), jnp.float32),
        in_specs=[pl.BlockSpec(memory_space=pltpu.SMEM)] * 2 + [pl.BlockSpec(memory_space=pl.ANY)] * 3,
        out_specs=pl.BlockSpec(memory_space=pl.ANY),
        scratch_shapes=[
            pltpu.VMEM((1 + 4 * SLOTS, BLK, BLK), jnp.bfloat16),
            pltpu.VMEM((1 + 4 * SLOTS, BLK, BLK), jnp.bfloat16),
            pltpu.VMEM((SLOTS, BLK, BLK), jnp.float32),
            pltpu.SemaphoreType.DMA((3,)),
            pltpu.SemaphoreType.DMA((SLOTS,)),
        ],
        name="sums",
    )(listed, spans, x, L, R)


def body(x_blocks, x_live, pair_slots, pair_count):
    x = x_blocks[0, 0]
    L, R, listed, spans = moves(x, x_live[0], pair_slots[0, 0], pair_count[0, 0])
    gram = sums(listed, spans, x, L.reshape(3 * SLOTS, BLK, BLK), R.reshape(4 * SLOTS, BLK, BLK))
    return gram[None, None]


def solution(mesh):
    return jax.shard_map(
        body,
        mesh=mesh,
        in_specs=(
            P("row", "col", None, None, None),
            P("row", "col", None),
            P("row", "col", None, None, None),
            P("row", "col", None),
        ),
        out_specs=P("row", "col", None, None, None),
        check_vma=False,
    )
```

time: 305 us -> 99.6 us (0.33); the launches traced: 301 us -> 98.6 us
  waiting for transfers between devices: 143 us -> 0 us
  matrix products: 126 us -> 0 us
  Pallas kernels: 0 us -> 97.3 us
  other arithmetic: 14.9 us -> 0 us
  starting transfers between devices: 12.8 us -> 0 us
    ppermute x14 -> x0, waiting for transfers between devices: 143 us -> none  [the longest x8 135 us: swapped_2(): lax.ppermute(value, axis, [(i, i ^ 1 << distance) for i in range(lax.axis...]
    dot_general x64 -> x0, matrix products: 126 us -> none  [the longest x16 62.5 us: one_block(): jnp.einsum('po,pij->oij', out_pick, product, precision=lax.Precision.HIGH...]
    pallas_call x0 -> x2, Pallas kernels: none -> 97.3 us  [the longest x1 83.4 us: moves(): pl.pallas_call(moves_kernel, out_shape=[jax.ShapeDtypeStruct((3,) + tile,...]
    ppermute x14 -> x0, starting transfers between devices: 12.8 us -> none  [the longest x8 9.66 us: swapped_2(): lax.ppermute(value, axis, [(i, i ^ 1 << distance) for i in range(lax.axis...]
    convert_element_type x17 -> x0, other arithmetic: 10.6 us -> none  [the longest x16 9.97 us: one_block(): weights = (positions < live_pairs).astype(jnp.float32)]
    select_n x4 -> x0, other arithmetic: 3.16 us -> none  [body(): mirrored = jnp.where(differ, swapped, mirrored)]
  transfers between devices with their start and end apart: 14 -> 0, of which waited for: 9 -> 0; matrix products, arithmetic and copies ran while one was open for 38% -> 0% of each run, Pallas kernels for 0% -> 0%
where the time goes in v1:
time: 99.6 us; the launch traced here: 98.6 us
  Pallas kernels  97.3 us (98%)
  local copies, waits for them, and re-layouts  1.32 us (1%)
    pallas_call x1, Pallas kernels, moves(): pl.pallas_call(moves_kernel, out_shape=[jax.ShapeDtypeStruct((3,) + tile,...  83.4 us
    pallas_call x1, Pallas kernels, sums(): pl.pallas_call(sums_kernel, out_shape=jax.ShapeDtypeStruct((SLOTS, BLK, B...  13.9 us

profile of v1, /device:TPU:239, one launch (start us, length us, event | category | flops | bytes accessed | tf_op | source)
XLA Modules:
  0.0 98.6 jit_solution(12121658500565051667)
XLA Ops:
  0.0 1.3 %copy.7 = s32[1,1,4,3,192]{4,3,2,1,0:T(4,128)} copy(s32[1,1,4,3,192]{4,2,3,1,0:T(4,128)} %param.6) | data formatting | bytes 18432 | tf_op args[2]
  1.3 83.4 %moves.1 = (bf16[3,16,128,128]{3,2,1,0:T(8,128)(2,1)}, bf16[4,16,128,128]{3,2,1,0:T(8,128)(2,1)}, s32[8,896]{1,0:T(8,128)}, s32[16,128]{1,0:T(8,128)}) custom-call(bf16[16,128,128]{2,1,0:T(8,128)(2,1)} %bitcast.9, s32[1,16]{1,0:T(1,128)} %bitcast.14, s32[4,3,192]{2,1,0:T(4,128)} %bitcast.13, s32[4]{0:T(128)} %bitcast.15), custom_call_target="tpu_custom_call" | custom-call | tf_op jit(solution)/shard_map/moves/pallas_call | solution.py:275
  84.7 13.9 %sums.1 = f32[16,128,128]{2,1,0:T(8,128)} custom-call(s32[8,896]{1,0:T(8,128)} %get-tuple-element.9.listed, s32[16,128]{1,0:T(8,128)} %get-tuple-element.10.spans, bf16[16,128,128]{2,1,0:T(8,128)(2,1)} %bitcast.10, bf16[48,128,128]{2,1,0:T(8,128)(2,1)} %bitcast.12, bf16[64,128,128]{2,1,0:T(8,128)(2,1)} %bitcast.11), custom_call_target="tpu_custom_call" | custom-call | tf_op jit(solution)/shard_map/sums/pallas_call | solution.py:345

commit v2 on v1

v2 whole, which is shorter than its diff:
```python
import functools

import jax
import jax.numpy as jnp
from jax import lax
from jax.experimental import pallas as pl
from jax.experimental.pallas import tpu as pltpu
from jax.sharding import PartitionSpec as P

SECTIONS = 4
SLOTS = 16
BLK = 128
PAIRS = 192
SIDE = 16
RING = 8
HALF = 8
CHUNKS = 4
NEAR = (0, 1, 2, 2, 0, 0, 0, 0)
GROUP = 4
LISTED = 896
GROUPS = 256
BATCH = 8
MESH = pl.DeviceIdType.MESH


def make_list(pairs, counts, left_live, right_live, listed, spans):
    slot_ids = lax.broadcasted_iota(jnp.int32, (SLOTS, PAIRS), 0)
    lanes = lax.broadcasted_iota(jnp.int32, (1, PAIRS), 1)
    earlier = (
        lax.broadcasted_iota(jnp.int32, (PAIRS, PAIRS), 0)
        < lax.broadcasted_iota(jnp.int32, (PAIRS, PAIRS), 1)
    ).astype(jnp.float32).astype(jnp.bfloat16)

    def hot(row):
        return (slot_ids == row).astype(jnp.float32)

    def look_up(live, row):
        table = jnp.broadcast_to(live.astype(jnp.float32), (8, SLOTS)).astype(jnp.bfloat16)
        return jnp.dot(
            table, hot(row).astype(jnp.bfloat16), preferred_element_type=jnp.float32
        )[0:1]

    chosen, places, totals = [], [], jnp.zeros((SLOTS, 1), jnp.float32)
    for s in range(SECTIONS):
        left, right, out = (pairs[k, s : s + 1, :] for k in range(3))
        used = look_up(left_live[s], left) * look_up(right_live[s], right)
        used = jnp.where(lanes < counts[s], used, 0.0)
        picked = hot(out) * used
        before = jnp.dot(picked.astype(jnp.bfloat16), earlier, preferred_element_type=jnp.float32)
        chosen.append(picked)
        places.append(before + totals)
        totals = totals + jnp.sum(picked, axis=1, keepdims=True)
    groups = jnp.floor((totals + (GROUP - 1)) * (1.0 / GROUP))
    below = (
        lax.broadcasted_iota(jnp.int32, (SLOTS, SLOTS), 1)
        < lax.broadcasted_iota(jnp.int32, (SLOTS, SLOTS), 0)
    ).astype(jnp.float32).astype(jnp.bfloat16)
    starts = jnp.dot(
        below,
        jnp.broadcast_to(groups, (SLOTS, BLK)).astype(jnp.bfloat16),
        preferred_element_type=jnp.float32,
    )
    lane = lax.broadcasted_iota(jnp.int32, (SLOTS, GROUPS), 1).astype(jnp.float32)
    slot = jnp.sum((lane >= starts[:, 0:1]).astype(jnp.float32), axis=0, keepdims=True) - 1.0
    total = jnp.sum(groups)
    spans[0:1, :] = jnp.where(lane[0:1] < total, slot, float(SLOTS)).astype(jnp.int32)
    spans[1:2, :] = jnp.full((1, GROUPS), total).astype(jnp.int32)
    first = starts[:, 0:1] * GROUP
    gathered = jnp.zeros((8, LISTED), jnp.float32)
    positions = lax.broadcasted_iota(jnp.int32, (LISTED, PAIRS), 0).astype(jnp.float32)
    row_ids = lax.broadcasted_iota(jnp.int32, (8, PAIRS), 0)
    for s in range(SECTIONS):
        place = jnp.sum(chosen[s] * (places[s] + first + 1.0), axis=0, keepdims=True) - 1.0
        codes = jnp.where(row_ids == 0, pairs[0, s : s + 1, :], pairs[1, s : s + 1, :]) + (1 + SLOTS * s)
        gathered += lax.dot_general(
            codes.astype(jnp.float32).astype(jnp.bfloat16),
            (positions == place).astype(jnp.float32).astype(jnp.bfloat16),
            (((1,), (1,)), ((), ())),
            preferred_element_type=jnp.float32,
        )
    listed[...] = gathered.astype(jnp.int32)


def moves_kernel(
    x, live, pairs, counts, L, R, X, Y, listed, spans,
    lv, rv, l_send, l_recv, r_send, r_recv, m_send, lv_send, lv_recv, rv_send, rv_recv, x_send, x_recv, y_send, y_recv, own_sem,
):
    a = lax.axis_index("row")
    b = lax.axis_index("col")

    def at(row, col):
        return (lax.rem(row + SIDE, SIDE), lax.rem(col + SIDE, SIDE))

    twin = a == b
    gap = lax.rem(lax.rem(b, RING) - lax.rem(a, RING) + RING, RING)
    back = lax.rem(RING - gap, RING)
    def any_of(value, options):
        found = value < 0
        for option in options:
            found = jnp.logical_or(found, value == option)
        return found

    late = any_of(back, [d for d in range(RING) if NEAR[d] >= 2])
    step = jnp.int32(0)
    for d in range(RING):
        step = jnp.where(back == d, NEAR[d], step)
    out_0, out_1, out_2 = (
        any_of(gap, [(d - j) % RING for d in range(RING) if NEAR[d] == j]) for j in range(3)
    )
    not_twin = jnp.logical_not(twin)
    go_0 = jnp.logical_and(out_0, not_twin)

    barrier = pltpu.get_barrier_semaphore()

    def hello(device):
        pl.semaphore_signal(barrier, inc=1, device_id=device, device_id_type=MESH)

    i = lax.rem(a, HALF)
    z = lax.rem(b, HALF)
    over_row = at(a + HALF, b)
    over_col = at(a, b + HALF)

    for k in range(1, 4):
        hello(at(a, b + k))
        hello(at(b, a + k))

    @pl.when(z == HALF - 1)
    def _():
        hello(at(a, b - HALF + 1))

    @pl.when(z == 0)
    def _():
        hello(over_col)

    for k in range(1, 4):
        hello(at(jnp.where(i + k >= HALF, a + k - HALF, a + k), b))

    @pl.when(i <= 2)
    def _():
        hello(over_row)

    @pl.when(not_twin)
    def _():
        hello(at(b, a))
        hello(at(b, a - step))

    one = jnp.int32(1)
    zero = jnp.int32(0)
    expected = (
        jnp.where(z == 0, jnp.int32(8), jnp.int32(6))
        + jnp.where(i <= 2, jnp.int32(4), jnp.int32(3))
        + jnp.where(not_twin, one, zero)
        + jnp.where(go_0, one, zero)
        + jnp.where(out_1, one, zero)
        + jnp.where(out_2, one, zero)
    )
    pl.semaphore_wait(barrier, expected)

    size = SLOTS // CHUNKS

    def part(q):
        return pl.ds(q * size, size)

    def remote(src, dst, send, recv, device):
        return pltpu.make_async_remote_copy(
            src_ref=src, dst_ref=dst, send_sem=send, recv_sem=recv, device_id=device, device_id_type=MESH
        )

    def left_src(k, q):
        return x.at[part(q)] if k == 0 else L.at[k - 1, part(q)]

    def left(k, q):
        return remote(left_src(k, q), L.at[k, part(q)], l_send.at[k, q], l_recv.at[k, q], at(a, b - 1))

    def left_over(k, q):
        return remote(left_src(k, q), Y.at[k, part(q)], l_send.at[k, q], y_recv.at[k, q], over_col)

    def left_after(k, q):
        return remote(Y.at[k, part(q)], L.at[k, part(q)], y_send.at[k, q], l_recv.at[k, q], at(a, b + HALF - 1))

    def start_left(k, q):
        if q % 2 == 0:
            left(k, q).start()
        else:
            @pl.when(z == 0)
            def _():
                left_over(k, q).start()

            @pl.when(z != 0)
            def _():
                left(k, q).start()

    def cross_left(k, q):
        if q % 2 == 1:
            @pl.when(z == 0)
            def _():
                left_over(k, q).wait_recv()
                left_after(k, q).start()

    def mirror(j, q):
        src = x.at[part(q)] if j == 0 else L.at[j - 1, part(q)]
        return remote(src, R.at[0, part(q)], m_send.at[j, q], r_recv.at[0, q], at(b + j, a))

    def right(k, q):
        return remote(R.at[0, part(q)], R.at[k, part(q)], r_send.at[k, q], r_recv.at[k, q], at(a - k, b))

    def right_over(q):
        return remote(R.at[0, part(q)], X.at[part(q)], x_send.at[3, q], x_recv.at[q], over_row)

    def right_after(k, q):
        return remote(X.at[part(q)], R.at[k, part(q)], x_send.at[k - 1, q], r_recv.at[k, q], at(a + HALF - k, b))

    def live_left(k):
        return remote(live, lv.at[k], lv_send.at[k], lv_recv.at[k], at(a, b - 1 - k))

    def live_mirror(k):
        return remote(live, rv.at[k], rv_send.at[k], rv_recv.at[k], at(b - k, a))

    own = pltpu.make_async_copy(x, R.at[0], own_sem)

    for k in range(3):
        live_left(k).start()
        live_mirror(k + 1).start()

    @pl.when(not_twin)
    def _():
        live_mirror(0).start()

    @pl.when(twin)
    def _():
        own.start()

    for q in range(CHUNKS):
        @pl.when(go_0)
        def _():
            mirror(0, q).start()

        start_left(0, q)

    def take_mirror(q):
        @pl.when(not_twin)
        def _():
            mirror(0, q).wait_recv()

        @pl.when(i <= 2)
        def _():
            right_over(q).start()

        for k in range(1, 4):
            @pl.when(i >= k)
            def _():
                right(k, q).start()

    def cross_right(q):
        @pl.when(i <= 2)
        def _():
            right_over(q).wait_recv()

            for k in range(1, 4):
                @pl.when(i < k)
                def _():
                    right_after(k, q).start()

    def take_and_cross(q):
        take_mirror(q)
        if q > 0:
            cross_right(q - 1)
        if q == CHUNKS - 1:
            cross_right(q)

    for q in range(CHUNKS):
        if q > 0:
            cross_left(0, q - 1)
        left(0, q).wait_recv()

        @pl.when(out_1)
        def _():
            mirror(1, q).start()

        start_left(1, q)
    cross_left(0, CHUNKS - 1)

    for k in range(3):
        live_left(k).wait_recv()
        live_mirror(k + 1).wait_recv()

    @pl.when(not_twin)
    def _():
        live_mirror(0).wait_recv()

    lefts = [live[...], lv[0], lv[1], lv[2]]
    rights = [jnp.where(twin, live[...], rv[0]), rv[1], rv[2], rv[3]]
    make_list(pairs, counts, lefts, rights, listed, spans)

    @pl.when(twin)
    def _():
        own.wait()

    for q in range(CHUNKS):
        cross_left(1, q)

        @pl.when(jnp.logical_not(late))
        def _():
            take_and_cross(q)

        left(1, q).wait_recv()

        @pl.when(out_2)
        def _():
            mirror(2, q).start()

        start_left(2, q)

    for q in range(CHUNKS):
        cross_left(2, q)

        @pl.when(late)
        def _():
            take_and_cross(q)

    for q in range(CHUNKS):
        left(2, q).wait_recv()
        for k in range(1, 4):
            right(k, q).wait_recv()

    for q in range(CHUNKS):
        for k in range(3):
            left(k, q).wait_send()
            if q % 2 == 1:
                @pl.when(z == 0)
                def _():
                    left_after(k, q).wait_send()

        for k in range(1, 4):
            @pl.when(i >= k)
            def _():
                right(k, q).wait_send()

            @pl.when(i < k)
            def _():
                right_after(k, q).wait_send()

        @pl.when(i <= 2)
        def _():
            right_over(q).wait_send()

        @pl.when(go_0)
        def _():
            mirror(0, q).wait_send()

        @pl.when(out_1)
        def _():
            mirror(1, q).wait_send()

        @pl.when(out_2)
        def _():
            mirror(2, q).wait_send()

    for k in range(3):
        live_left(k).wait_send()
        live_mirror(k + 1).wait_send()

    @pl.when(not_twin)
    def _():
        live_mirror(0).wait_send()


def moves(x, live, pairs, counts):
    dma = pltpu.SemaphoreType.DMA
    tile = (SLOTS, BLK, BLK)
    return pl.pallas_call(
        moves_kernel,
        out_shape=[
            jax.ShapeDtypeStruct((3,) + tile, jnp.bfloat16),
            jax.ShapeDtypeStruct((4,) + tile, jnp.bfloat16),
            jax.ShapeDtypeStruct(tile, jnp.bfloat16),
            jax.ShapeDtypeStruct((3,) + tile, jnp.bfloat16),
            jax.ShapeDtypeStruct((8, LISTED), jnp.int32),
            jax.ShapeDtypeStruct((8, GROUPS), jnp.int32),
        ],
        in_specs=[
            pl.BlockSpec(memory_space=pl.ANY),
            pl.BlockSpec(memory_space=pltpu.VMEM),
            pl.BlockSpec(memory_space=pltpu.VMEM),
            pl.BlockSpec(memory_space=pltpu.SMEM),
        ],
        out_specs=[
            pl.BlockSpec(memory_space=pl.ANY),
            pl.BlockSpec(memory_space=pl.ANY),
            pl.BlockSpec(memory_space=pl.ANY),
            pl.BlockSpec(memory_space=pl.ANY),
            pl.BlockSpec(memory_space=pltpu.VMEM),
            pl.BlockSpec(memory_space=pltpu.VMEM),
        ],
        scratch_shapes=[
            pltpu.VMEM((3, 1, SLOTS), jnp.int32),
            pltpu.VMEM((4, 1, SLOTS), jnp.int32),
            dma((3, CHUNKS)), dma((3, CHUNKS)),
            dma((4, CHUNKS)), dma((4, CHUNKS)),
            dma((3, CHUNKS)),
            dma((3,)), dma((3,)), dma((4,)), dma((4,)),
            dma((4, CHUNKS)), dma((CHUNKS,)), dma((3, CHUNKS)), dma((3, CHUNKS)),
            dma,
        ],
        compiler_params=pltpu.CompilerParams(collective_id=0, has_side_effects=True),
        name="moves",
    )(x, live, pairs, counts)


def sums_kernel(listed, spans, x, L, R, out, left, right, total, in_sems, out_sem):
    copies = [
        pltpu.make_async_copy(x, left.at[pl.ds(1, SLOTS)], in_sems.at[0]),
        pltpu.make_async_copy(L, left.at[pl.ds(1 + SLOTS, 3 * SLOTS)], in_sems.at[1]),
        pltpu.make_async_copy(R, right.at[pl.ds(1, 4 * SLOTS)], in_sems.at[2]),
    ]
    for c in copies:
        c.start()
    left[0] = jnp.zeros((BLK, BLK), jnp.bfloat16)
    right[0] = jnp.zeros((BLK, BLK), jnp.bfloat16)
    for c in copies:
        c.wait()

    for o in range(SLOTS):
        total[o] = jnp.zeros((BLK, BLK), jnp.float32)

    def batch(i, carry):
        for u in range(BATCH):
            group = i * BATCH + u
            base = group * GROUP
            product = None
            for k in range(0, GROUP, GROUP):
                rows = jnp.concatenate([left[listed[0, base + n]] for n in range(GROUP)], axis=1)
                cols = jnp.concatenate([right[listed[1, base + n]] for n in range(GROUP)], axis=1)
                term = lax.dot_general(
                    rows, cols, (((1,), (1,)), ((), ())), preferred_element_type=jnp.float32
                )
                product = term if product is None else product + term
            total[spans[0, group]] += product
        return carry

    lax.fori_loop(0, lax.div(spans[1, 0] + (BATCH - 1), BATCH), batch, 0)
    done = pltpu.make_async_copy(total.at[pl.ds(0, SLOTS)], out, out_sem)
    done.start()
    done.wait()


def sums(listed, spans, x, L, R):
    return pl.pallas_call(
        sums_kernel,
        out_shape=jax.ShapeDtypeStruct((SLOTS, BLK, BLK), jnp.float32),
        in_specs=[pl.BlockSpec(memory_space=pltpu.SMEM)] * 2 + [pl.BlockSpec(memory_space=pl.ANY)] * 3,
        out_specs=pl.BlockSpec(memory_space=pl.ANY),
        scratch_shapes=[
            pltpu.VMEM((1 + 4 * SLOTS, BLK, BLK), jnp.bfloat16),
            pltpu.VMEM((1 + 4 * SLOTS, BLK, BLK), jnp.bfloat16),
            pltpu.VMEM((SLOTS + 1, BLK, BLK), jnp.float32),
            pltpu.SemaphoreType.DMA((3,)),
            pltpu.SemaphoreType.DMA,
        ],
        name="sums",
    )(listed, spans, x, L, R)


def body(x_blocks, x_live, pair_slots, pair_count):
    x = x_blocks[0, 0]
    L, R, _, _, listed, spans = moves(x, x_live[0], jnp.swapaxes(pair_slots[0, 0], 0, 1), pair_count[0, 0])
    gram = sums(listed, spans, x, L.reshape(3 * SLOTS, BLK, BLK), R.reshape(4 * SLOTS, BLK, BLK))
    return gram[None, None]


def solution(mesh):
    return jax.shard_map(
        body,
        mesh=mesh,
        in_specs=(
            P("row", "col", None, None, None),
            P("row", "col", None),
            P("row", "col", None, None, None),
            P("row", "col", None),
        ),
        out_specs=P("row", "col", None, None, None),
        check_vma=False,
    )
```

time: 99.6 us -> 82.6 us (0.83)
  the two profiles are of different devices: /device:TPU:239 before, /device:TPU:227 now
where the time goes in v2:
time: 82.6 us; the launch traced here: 81.1 us
  Pallas kernels  81.1 us (98%)
    pallas_call x1, Pallas kernels, moves(): pl.pallas_call(moves_kernel, out_shape=[jax.ShapeDtypeStruct((3,) + tile,...  73.4 us
    pallas_call x1, Pallas kernels, sums(): pl.pallas_call(sums_kernel, out_shape=jax.ShapeDtypeStruct((SLOTS, BLK, B...  7.7 us

profile of v2, /device:TPU:227, one launch (start us, length us, event | category | flops | bytes accessed | tf_op | source)
XLA Modules:
  0.0 81.1 jit_solution(1195734069946729718)
XLA Ops:
  0.0 73.4 %moves.1 = (bf16[3,16,128,128]{3,2,1,0:T(8,128)(2,1)}, bf16[4,16,128,128]{3,2,1,0:T(8,128)(2,1)}, bf16[16,128,128]{2,1,0:T(8,128)(2,1)}, bf16[3,16,128,128]{3,2,...) custom-call(bf16[16,128,128]{2,1,0:T(8,128)(2,1)} %bitcast.9, s32[1,16]{1,0:T(1,128)} %bitcast.14, ...), custom_call_target="tpu_custom_call" | custom-call | tf_op jit(solution)/shard_map/moves/pallas_call | solution.py:371
  73.4 7.7 %sums.1 = f32[16,128,128]{2,1,0:T(8,128)} custom-call(s32[8,896]{1,0:T(8,128)} %get-tuple-element.9.listed, s32[8,256]{1,0:T(8,128)} %get-tuple-element.10.spans, bf16[16,128,128]{2,1,0:T(8,128)(2,1)} %bitcast.10, bf16[48,128,128]{2,1,0:T(8,128)(2,1)} %bitcast.12, bf16[64,128,128]{2,1,0:T(8,128)(2,1)} %bitcast.11), custom_call_target="tpu_custom_call" | custom-call | tf_op jit(solution)/shard_map/sums/pallas_call | solution.py:448
